TPU v7x, 512 devices: a whole 4x4x16 slice. The times are simulated.
512 devices in a mesh: teach: 16 (over x, y), stud: 8 (over z_lo, core), mdl: 4 (over z_hi).
Axes of the slice: x: 4, y: 4, z: 16 (z_hi: 4, z_lo: 4; z = z_hi * 4 + z_lo), core: 2. Of those that a mesh axis runs over, the one named last changes fastest.
Arguments:
- states: bfloat16 [16384, 512], P(('teach', 'stud')), may hold values from -6 to 6
- task_ids: int32 [16384, 1], P(('teach', 'stud')), may hold values from 0 to 15; in each aligned block of 128 rows (0 to 127, 128 to 255, ...) at most 12 rows name the same one
- student_batch: int32 [16384, 1], P(('teach', 'stud')), may hold values from 0 to 127; in each aligned block of 128 rows (0 to 127, 128 to 255, ...) at most 2 rows name the same one
- teach_in: bfloat16 [16, 512, 1024], P('teach', None, 'mdl'), may hold values from -0.25 to 0.25
- teach_out: bfloat16 [16, 1024, 512], P('teach', 'mdl'), may hold values from -0.1875 to 0.1875
- student_up: bfloat16 [512, 1024], P(None, 'mdl'), may hold values from -0.25 to 0.25
- student_down: bfloat16 [512, 1024], P(None, 'mdl'), may hold values from -0.1875 to 0.1875
Outputs:
- grad_up: float32 [512, 1024], P(('teach', 'stud'), 'mdl')
- grad_down: float32 [512, 1024], P(('teach', 'stud'), 'mdl')
Inputs may be any that keep to these rules, and one draw needn't show every extreme that they name: `task_ids`: teacher t lives at index t // 1 of teach. Among one device's 128 states no teacher is named more than 12 times, and in every draw some teacher is named exactly 12 times there; every teacher is named somewhere. `student_batch`: batch b belongs to teach index b // 8 and stud index b % 8. Among one device's 128 states no batch is named more than 2 times, some batch exactly 2 times; every batch holds one state or more.
All inputs are finite; a program needn't handle non-finite values.
Results may differ from a plain program's by a relative error of at most 0.0023.
Values may be sent and summed in bfloat16 or wider, within the bound.
A program may use at most 64 MiB of HBM per device.

v0:
```python
import jax
import jax.numpy as jnp
from jax import lax
from jax.sharding import PartitionSpec as P


def silu_slope(value):
    sig = jax.nn.sigmoid(value)
    return sig * (1.0 + value * (1.0 - sig))


def slot_table(labels_of, groups, capacity):
    onehot = (labels_of[:, None] == jnp.arange(groups, dtype=jnp.int32)[None, :]).astype(jnp.int32)
    before = jnp.sum((jnp.cumsum(onehot, axis=0) - onehot) * onehot, axis=1)
    slot_index = labels_of * capacity + before
    return (slot_index[None, :] == jnp.arange(groups * capacity, dtype=jnp.int32)[:, None]).astype(
        jnp.float32
    )


def on_device(states, task_ids, student_batch, teach_in, teach_out, student_up, student_down):
    row_count = states.shape[0]
    width = states.shape[1]
    owners = lax.axis_size("teach")
    local_teachers = teach_in.shape[0]
    teachers = owners * local_teachers
    batches = lax.axis_size(("teach", "stud"))
    teach_room = 3 * row_count // (2 * teachers)
    batch_room = 2 * row_count // batches
    action_width = teach_out.shape[2]
    dispatch = slot_table(task_ids[:, 0], teachers, teach_room)
    outgoing = jnp.dot(
        dispatch.astype(jnp.bfloat16), states, preferred_element_type=jnp.float32
    ).astype(jnp.bfloat16)
    outgoing = outgoing.reshape(owners, local_teachers, teach_room, width)
    hidden = jnp.einsum(
        "ntcd,tdh->ntch",
        lax.all_to_all(outgoing, "teach", split_axis=0, concat_axis=0, tiled=True),
        teach_in,
        preferred_element_type=jnp.float32,
    )
    hidden = jax.nn.silu(hidden).astype(jnp.bfloat16)
    partial_labels = jnp.einsum(
        "ntch,tha->ntca", hidden, teach_out, preferred_element_type=jnp.float32
    )
    partial_labels = lax.psum(partial_labels, "mdl")
    returned = lax.all_to_all(partial_labels, "teach", split_axis=0, concat_axis=0, tiled=True)
    targets = jnp.dot(
        dispatch.T,
        returned.reshape(-1, action_width),
        precision=lax.Precision.HIGHEST,
        preferred_element_type=jnp.float32,
    )
    batch_list = student_batch[:, 0]
    sending = slot_table(batch_list, batches, batch_room)
    rows_out = jnp.dot(
        sending.astype(jnp.bfloat16), states, preferred_element_type=jnp.float32
    ).astype(jnp.bfloat16)
    goals_out = jnp.dot(
        sending, targets, precision=lax.Precision.HIGHEST, preferred_element_type=jnp.float32
    )
    valid_out = jnp.sum(sending, axis=1)
    rows_in, goals_in, valid_in = (
        lax.all_to_all(
            rows_out.reshape(batches, batch_room, width).astype(jnp.float32),
            ("teach", "stud"),
            split_axis=0,
            concat_axis=0,
            tiled=True,
        ).astype(jnp.bfloat16),
        lax.all_to_all(
            goals_out.reshape(batches, batch_room, action_width),
            ("teach", "stud"),
            split_axis=0,
            concat_axis=0,
            tiled=True,
        ),
        lax.all_to_all(
            valid_out.reshape(batches, batch_room),
            ("teach", "stud"),
            split_axis=0,
            concat_axis=0,
            tiled=True,
        ),
    )
    rows_used = rows_in.reshape(-1, width)
    goals = goals_in.reshape(-1, action_width)
    valid = valid_in.reshape(-1)
    weight = valid * (2.0 / jnp.sum(valid))
    pre = jnp.dot(rows_used, student_up, preferred_element_type=jnp.float32)
    act = jax.nn.silu(pre).astype(jnp.bfloat16)
    partial_pred = jnp.einsum("rh,ah->ra", act, student_down, preferred_element_type=jnp.float32)
    error = lax.psum(partial_pred, "mdl") - goals
    scaled = (error * weight[:, None]).astype(jnp.bfloat16)
    grad_down = jnp.einsum("ra,rh->ah", scaled, act, preferred_element_type=jnp.float32)
    back = jnp.dot(scaled, student_down, preferred_element_type=jnp.float32)
    pre_grad = (back * silu_slope(pre)).astype(jnp.bfloat16)
    grad_up = jnp.einsum("rd,rh->dh", rows_used, pre_grad, preferred_element_type=jnp.float32)
    share_up, share_down = (
        lax.psum_scatter(grad_up, ("teach", "stud"), scatter_dimension=0, tiled=True),
        lax.psum_scatter(grad_down, ("teach", "stud"), scatter_dimension=0, tiled=True),
    )
    return (share_up, share_down)


def solution(mesh):
    in_specs = (
        P(("teach", "stud"), None),
        P(("teach", "stud"), None),
        P(("teach", "stud"), None),
        P("teach", None, "mdl"),
        P("teach", "mdl", None),
        P(None, "mdl"),
        P(None, "mdl"),
    )
    out_specs = (P(("teach", "stud"), "mdl"), P(("teach", "stud"), "mdl"))
    return jax.shard_map(
        on_device, mesh=mesh, in_specs=in_specs, out_specs=out_specs, check_vma=False
    )
```

profile of v0, /device:TPU:1, one launch (start us, length us, event | category | flops | bytes accessed | tf_op | source)
XLA Modules:
  0.0 1540.4 jit_solution(16467876364999906796)
XLA Ops:
  7.2 0.7 copy-done.4
  7.9 0.1 fusion.28
  8.0 0.2 reduce_window_sum.23
  8.1 0.2 select_reduce_fusion
  8.3 0.5 copy-done.1
  8.8 0.2 convolution_convert_fusion.1
  9.0 0.7 reshape.66
  9.7 7.6 all-to-all-start.1
  17.3 0.6 copy-done.5
  18.0 0.1 fusion.31
  18.1 0.2 reduce_window_sum.22
  18.2 0.2 select_reduce_fusion.1
  18.4 0.2 fusion
  18.6 0.8 reshape.74
  19.4 5.2 all-to-all-done.1
  24.7 11.0 all-to-all-start
  35.7 0.0 all-reduce.9.cloned.1.call-start
  35.8 1.2 convolution_bitcast_fusion
  37.0 11.9 all-to-all-done
  48.9 0.1 reshape.65
  49.0 0.2 fusion.38
  49.3 1.1 fusion.37
  50.3 0.0 all-reduce.9.cloned.1.call-update
  50.4 104.0 %all-reduce.9.cloned.1.call-done = (f32[256,512]{1,0:T(8,128)}, f32[16,1,12,512]{3,0,2,1:T(8,128)}) async-done(((f32[256,512]{1,0:T(8,128)}, f32[16,1,12,512]{3,0,2,1:T(8,128)}), (f32[256,512]{1,0:T(8,128)}, f32[16,1,12,512]{3,0,2,1:T(8,128)})) %all-reduce.9.cloned.1.call-update) | async-done | bytes 917520 | tf_op jit(solution)/shard_map/psum | solution.py:93
  154.3 2.2 copy.22
  156.5 6.2 all-to-all-start.2
  162.7 0.1 convert_reduce_fusion
  162.8 0.8 all_to_all.22
  163.6 7.2 all-to-all-done.2
  170.8 10.2 all-to-all-start.4
  181.0 0.9 reduce.2
  182.0 0.3 fusion.27
  182.4 0.4 fusion.25
  182.8 1.1 reshape.72
  183.9 6.9 all-to-all-done.4
  190.8 6.2 all-to-all-start.3
  197.0 0.0 all-reduce.7.cloned.1.call-start
  197.1 0.7 reduce_sum.39
  198.5 0.2 multiply_reduce_fusion
  198.7 0.1 mul.74
  198.9 16.5 %all-to-all-done.3 = f32[128,2,512]{2,1,0:T(2,128)S(1)} async-done(((f32[128,2,512]{2,1,0:T(2,128)}), f32[128,2,512]{2,1,0:T(2,128)S(1)}, u32[]{:S(2)}, u32[]{:S(2)}) %all-to-all-start.3) | async-done | bytes 524320 | tf_op jit(solution)/shard_map/all_to_all | solution.py:71
  215.3 0.4 reshape.73
  215.7 0.1 multiply_convert_fusion
  215.8 1.4 fusion.2
  217.1 1.1 fusion.36
  218.3 1.3 dynamic-slice
  220.2 1312.1 %all-reduce.7.cloned.1.call-done = (f32[512,256]{1,0:T(8,128)}, f32[512,256]{1,0:T(8,128)}) async-done(((f32[512,256]{1,0:T(8,128)}, f32[512,256]{1,0:T(8,128)}), (f32[512,256]{1,0:T(8,128)}, f32[512,256]{1,0:T(8,128)})) %all-reduce.7.cloned.1.call-update) | async-done | bytes 1048592
  1532.3 1.3 constant_dynamic-slice_fusion
  (17 shorter events, 0.1 us)
Async XLA Ops:
  7.2 42.1 %copy-start = (bf16[512,256]{1,0:T(8,128)(2,1)S(1)}, bf16[512,256]{1,0:T(8,128)(2,1)}, u32[]{:S(2)}) copy-start(bf16[512,256]{1,0:T(8,128)(2,1)} %param.13) | copy-start | bytes 786436
  7.2 0.7 copy-start.4
  7.9 0.9 copy-start.1
  9.7 14.9 all-to-all-start.1
  17.3 0.7 copy-start.5
  19.4 16.3 %copy-start.6 = (bf16[1,256,512]{2,1,0:T(8,128)(2,1)S(1)}, bf16[1,256,512]{2,1,0:T(8,128)(2,1)}, u32[]{:S(2)}) copy-start(bf16[1,256,512]{2,1,0:T(8,128)(2,1)} %param.11) | copy-start | bytes 786436
  19.4 16.3 %copy-start.7 = (bf16[1,512,256]{2,1,0:T(8,128)(2,1)S(1)}, bf16[1,512,256]{2,1,0:T(8,128)(2,1)}, u32[]{:S(2)}) copy-start(bf16[1,512,256]{2,1,0:T(8,128)(2,1)} %param.10) | copy-start | bytes 786436
  24.7 24.2 %all-to-all-start = ((bf16[128,2,512]{2,1,0:T(2,128)(2,1)}), bf16[128,2,512]{2,1,0:T(2,128)(2,1)S(1)}, u32[]{:S(2)}, u32[]{:S(2)}) async-start(bf16[128,2,512]{2,1,0:T(2,128)(2,1)} %reshape.74), calls=%async_computation | async-start | bytes 524288 | tf_op jit(solution)/shard_map/all_to_all | solution.py:64
  35.7 118.6 %all-reduce.9.cloned.1.call-start = ((), (), s32[]{:S(2)}) async-start(), calls=%async_computation.6 | async-start | bytes 1835008 | tf_op jit(solution)/shard_map/psum | solution.py:93
  37.0 12.0 copy-start.3
  156.5 14.3 all-to-all-start.2
  170.8 20.0 %all-to-all-start.4 = ((f32[128,1,2]{2,1,0:T(1,128)}), f32[128,1,2]{2,1,0:T(1,128)S(1)}, u32[]{:S(2)}, u32[]{:S(2)}) async-start(f32[128,1,2]{2,1,0:T(1,128)} %bitcast.17), calls=%async_computation.4 | async-start | bytes 131072 | tf_op jit(solution)/shard_map/all_to_all | solution.py:78
  190.8 24.5 %all-to-all-start.3 = ((f32[128,2,512]{2,1,0:T(2,128)}), f32[128,2,512]{2,1,0:T(2,128)S(1)}, u32[]{:S(2)}, u32[]{:S(2)}) async-start(f32[128,2,512]{2,1,0:T(2,128)} %reshape.72), calls=%async_computation.3 | async-start | bytes 1048576 | tf_op jit(solution)/shard_map/all_to_all | solution.py:71
  197.0 1335.2 %all-reduce.7.cloned.1.call-start = ((), (), s32[]{:S(2)}) async-start(), calls=%async_computation.5 | async-start | bytes 2097152
  198.8 16.8 %copy-start.2 = (f32[256,512]{1,0:T(8,128)S(1)}, f32[256,512]{1,0:T(8,128)}, u32[]{:S(2)}) copy-start(f32[256,512]{1,0:T(8,128)} %get-tuple-element.4) | copy-start | bytes 1572868
Sparse Core Ops, SparseCore 0:
  50.5 103.7 all-reduce.8
  218.4 1313.8 all-reduce.6
where the time goes:
time: 1550 us; the launch traced here: 1540 us
  waiting for transfers between devices  1460 us (94%)
  starting transfers between devices  41.4 us (3%)
  between operations  15.6 us (1%)
    unnamed x3, waiting for transfers between devices  1310 us
    psum x1, waiting for transfers between devices, on_device(): error = lax.psum(partial_pred, 'mdl') - goals  104 us
  transfers between devices with their start and end apart: 7, of which 7 were waited for; matrix products, arithmetic and copies ran while one was open for 1% of the time, Pallas kernels for 0%

commit v1 on v0

v1 whole, which is shorter than its diff:
```python
import functools
import math

import jax
import jax.numpy as jnp
from jax import lax
from jax.experimental import pallas as pl
from jax.experimental.pallas import tpu as pltpu
from jax.sharding import PartitionSpec as P

MESH = pl.DeviceIdType.MESH
F32, BF16, I32 = jnp.float32, jnp.bfloat16, jnp.int32
ROOM = 12
BLOCK = 16
LANES = 128


def dot(a, b, ca=1, cb=0):
    return lax.dot_general(a, b, (((ca,), (cb,)), ((), ())), preferred_element_type=F32)


def iota(shape, dim):
    return lax.broadcasted_iota(I32, shape, dim)


def onehot(mask):
    return jnp.where(mask, 1.0, 0.0).astype(BF16)


def silu(value):
    return value * jax.nn.sigmoid(value)


def silu_slope(value):
    sig = jax.nn.sigmoid(value)
    return sig * (1.0 + value * (1.0 - sig))


def kernel(
    side,
    teachers,
    studs,
    states,
    tasks,
    batches,
    teach_in,
    teach_out,
    up,
    down,
    grad_up,
    grad_down,
    out,
    got,
    x,
    hid,
    act,
    pre,
    err,
    first_out,
    first_in,
    second_out,
    second_in,
    hist_out,
    hist_in,
    part_out,
    part_in,
    last_out,
    last_in,
    go_s,
    go_r,
    sum_s,
    sum_r,
    hist_s,
    hist_r,
    part_s,
    part_r,
    last_s,
    last_r,
):
    me_t, me_s, me_m = lax.axis_index("teach"), lax.axis_index("stud"), lax.axis_index("mdl")
    my_x, my_y = me_t // side, me_t % side
    rows, width = states.shape
    slots, used = teachers * BLOCK, teachers * ROOM
    pieces = width // LANES
    mates = (me_m + 1 - 2 * (me_m % 2), 3 - me_m)

    def hops(step):
        dx, dy = step // side, step % side
        return min(dx, side - dx) + min(dy, side - dy)

    steps = sorted(range(1, teachers), key=lambda step: -hops(step))

    def peer(step):
        return ((my_x + step // side) % side) * side + (my_y + step % side) % side

    barrier = pltpu.get_barrier_semaphore()
    for step in steps:
        pl.semaphore_signal(barrier, inc=1, device_id={"teach": peer(step)}, device_id_type=MESH)
    for step in range(1, studs):
        pl.semaphore_signal(
            barrier, inc=1, device_id={"stud": (me_s + step) % studs}, device_id_type=MESH
        )
    for mate in mates:
        pl.semaphore_signal(barrier, inc=1, device_id={"mdl": mate}, device_id_type=MESH)

    def send(src, dst, send_sem, recv_sem, where):
        copy = pltpu.make_async_remote_copy(
            src_ref=src,
            dst_ref=dst,
            send_sem=send_sem,
            recv_sem=recv_sem,
            device_id=where,
            device_id_type=MESH,
        )
        return copy

    hot = jnp.where(tasks[...] == iota((rows, teachers), 1), 1.0, 0.0)
    lower = onehot(iota((rows, rows), 0) > iota((rows, rows), 1))
    before = jnp.sum(dot(lower, hot.astype(BF16)) * hot, axis=1, keepdims=True)
    slot = tasks[...].astype(F32) * BLOCK + before
    slot = jnp.transpose(jnp.broadcast_to(slot, (rows, rows)))[0:1, :].astype(I32)
    note = ((slot >> 4) * BLOCK + ROOM + 1 + ((slot & 15) >> 2)) * 4 + (slot & 3)
    place = iota((slots, rows), 0)
    batch_hot = onehot(batches[...] == iota((rows, LANES), 1))
    dispatch = onehot(place == slot)
    for piece in range(pieces):
        noted = place * 4 + piece == note
        if piece == 0:
            noted = noted | ((place & 15) == ROOM)
        cols = slice(piece * LANES, (piece + 1) * LANES)
        block = dot(dispatch, states[:, cols]) + dot(onehot(noted), batch_hot)
        out[:, :, cols] = block.astype(BF16).reshape(teachers, BLOCK, LANES)

    pl.semaphore_wait(barrier, teachers - 1 + studs - 1 + 2)

    going = []
    for step in steps:
        to = peer(step)
        copy = send(
            out.at[to], got.at[me_t], go_s.at[step], go_r.at[step], {"teach": to}
        )
        copy.start()
        going.append(copy)
    got[me_t] = out[me_t]

    source = iota((used, slots), 1)
    target = iota((used, slots), 0)
    base, inner = (source >> 4) * ROOM, source & 15
    keep = onehot((target == base + inner) & (inner < ROOM))

    for copy in going:
        copy.wait_recv()

    arrived = got[...].reshape(slots, width)
    x[...] = dot(keep, arrived).astype(BF16)
    hid[...] = silu(dot(x[...], teach_in[0])).astype(BF16)
    pre[...] = dot(x[...], up[...])
    act[...] = silu(pre[...]).astype(BF16)

    order, firsts, seconds = [], [], []
    for turn in range(4):
        chunk = (my_x * 4 // side + 1 + turn) % 4
        cols = pl.ds(pl.multiple_of(chunk * LANES, LANES), LANES)
        order.append((chunk, cols))
        diff = dot(act[...], down[cols, :], 1, 1) - dot(hid[...], teach_out[0, :, cols])
        err[turn] = diff
        first_out[turn] = diff.astype(BF16)
        copy = send(
            first_out.at[turn],
            first_in.at[turn],
            sum_s.at[0, turn],
            sum_r.at[0, turn],
            {"mdl": mates[turn % 2]},
        )
        copy.start()
        firsts.append(copy)

    marks = onehot((iota((8, slots), 1) & 15) == ROOM)
    hist_out[...] = dot(marks, arrived[:, :LANES])
    hists = []
    for step in range(1, studs):
        to = (me_s + step) % studs
        copy = send(
            hist_out, hist_in.at[me_s], hist_s.at[step], hist_r.at[step], {"stud": to}
        )
        copy.start()
        hists.append(copy)
    hist_in[me_s] = hist_out[...]
    batch_of = jnp.zeros((used, LANES), F32)
    for piece in range(pieces):
        pick = onehot((target == base + (inner - ROOM - 1) * 4 + piece) & (inner > ROOM))
        batch_of += dot(pick, arrived[:, piece * LANES : (piece + 1) * LANES])
    pre[...] = silu_slope(pre[...])

    for turn in range(4):
        firsts[turn].wait_recv()
        diff = err[turn] + first_in[turn].astype(F32)
        err[turn] = diff
        second_out[turn] = diff.astype(BF16)
        copy = send(
            second_out.at[turn],
            second_in.at[turn],
            sum_s.at[1, turn],
            sum_r.at[1, turn],
            {"mdl": mates[1 - turn % 2]},
        )
        copy.start()
        seconds.append(copy)

    for copy in hists:
        copy.wait_recv()
    counts = jnp.sum(hist_in[...], axis=0)
    share = jnp.where(counts > 0.0, 2.0 / jnp.maximum(counts, 1.0), 0.0)
    weight = jnp.sum(batch_of * share[0:1, :], axis=1, keepdims=True)

    def part_copy(kind, to):
        return send(
            part_out.at[kind, to],
            part_in.at[kind, me_t],
            part_s.at[kind, to],
            part_r.at[kind, me_t],
            {"teach": to},
        )

    per = teachers // 4
    part_rows = part_out.shape[2]
    back = jnp.zeros((used, up.shape[1]), F32)
    for turn in range(4):
        chunk, cols = order[turn]
        seconds[turn].wait_recv()
        total = err[turn] + second_in[turn].astype(F32)
        scaled = (total * weight).astype(BF16)
        grad = dot(scaled, act[...], 0, 0)
        part_out[1, pl.ds(chunk * per, per)] = grad.astype(BF16).reshape(per, part_rows, -1)
        back += dot(scaled, down[cols, :])
        for piece in range(per):
            to = chunk * per + piece

            @pl.when(to != me_t)
            def _():
                part_copy(1, to).start()

    pre_grad = (back * pre[...]).astype(BF16)
    grad = dot(x[...], pre_grad, 0, 0)
    part_out[0] = grad.astype(BF16).reshape(teachers, part_rows, -1)
    for step in steps:
        part_copy(0, peer(step)).start()
    part_in[1, me_t] = part_out[1, me_t]
    part_in[0, me_t] = part_out[0, me_t]

    def part_wait(kind):
        for step in steps:
            source = peer(step)
            send(
                part_out.at[kind, source],
                part_in.at[kind, source],
                part_s.at[kind, source],
                part_r.at[kind, source],
                {"teach": source},
            ).wait_recv()
        return jnp.sum(part_in[kind].astype(F32), axis=0)

    chips = studs // 2
    sum_down = part_wait(1).reshape(chips, part_rows // chips, -1)
    sum_up = part_wait(0).reshape(chips, part_rows // chips, -1)
    last_out[...] = jnp.concatenate([sum_up, sum_down], axis=1).astype(BF16)
    lasts = []
    for step in range(1, studs):
        to = (me_s + step) % studs
        copy = send(
            last_out.at[to // 2],
            last_in.at[me_s],
            last_s.at[step],
            last_r.at[step],
            {"stud": to},
        )
        copy.start()
        lasts.append(copy)
    last_in[me_s] = last_out[me_s // 2]
    for copy in lasts:
        copy.wait_recv()
    total = jnp.sum(last_in[...].astype(F32), axis=0)
    mine = grad_up.shape[0]
    even = jnp.full(grad_up.shape, me_s % 2, I32) == 0
    grad_up[...] = jnp.where(even, total[0:mine], total[mine : 2 * mine])
    grad_down[...] = jnp.where(even, total[2 * mine : 3 * mine], total[3 * mine : 4 * mine])

    for copy in going + firsts + hists + seconds + lasts:
        copy.wait_send()
    for step in steps:
        for kind in range(2):
            part_copy(kind, peer(step)).wait_send()


def solution(mesh):
    teachers, studs = mesh.shape["teach"], mesh.shape["stud"]
    side = math.isqrt(teachers)

    def on_device(states, tasks, batches, teach_in, teach_out, up, down):
        width, part = up.shape
        actions = down.shape[0]
        slots, used = teachers * BLOCK, teachers * ROOM
        mine = width // (teachers * studs)
        vmem = pl.BlockSpec(memory_space=pltpu.VMEM)
        result = jax.ShapeDtypeStruct((mine, part), F32)
        dma = pltpu.SemaphoreType.DMA
        return pl.pallas_call(
            functools.partial(kernel, side, teachers, studs),
            out_shape=(result, result),
            in_specs=[vmem] * 7,
            out_specs=(vmem, vmem),
            scratch_shapes=[
                pltpu.VMEM((teachers, BLOCK, width), BF16),
                pltpu.VMEM((teachers, BLOCK, width), BF16),
                pltpu.VMEM((used, width), BF16),
                pltpu.VMEM((used, part), BF16),
                pltpu.VMEM((used, part), BF16),
                pltpu.VMEM((used, part), F32),
                pltpu.VMEM((4, used, actions // 4), F32),
                pltpu.VMEM((4, used, actions // 4), BF16),
                pltpu.VMEM((4, used, actions // 4), BF16),
                pltpu.VMEM((4, used, actions // 4), BF16),
                pltpu.VMEM((4, used, actions // 4), BF16),
                pltpu.VMEM((8, LANES), F32),
                pltpu.VMEM((studs, 8, LANES), F32),
                pltpu.VMEM((2, teachers, width // teachers, part), BF16),
                pltpu.VMEM((2, teachers, width // teachers, part), BF16),
                pltpu.VMEM((studs // 2, 4 * mine, part), BF16),
                pltpu.VMEM((studs, 4 * mine, part), BF16),
                dma((teachers,)),
                dma((teachers,)),
                dma((2, 4)),
                dma((2, 4)),
                dma((studs,)),
                dma((studs,)),
                dma((2, teachers)),
                dma((2, teachers)),
                dma((studs,)),
                dma((studs,)),
            ],
            compiler_params=pltpu.CompilerParams(collective_id=0, has_side_effects=True),
        )(states, tasks, batches, teach_in, teach_out, up, down)

    in_specs = (
        P(("teach", "stud"), None),
        P(("teach", "stud"), None),
        P(("teach", "stud"), None),
        P("teach", None, "mdl"),
        P("teach", "mdl", None),
        P(None, "mdl"),
        P(None, "mdl"),
    )
    out_specs = (P(("teach", "stud"), "mdl"), P(("teach", "stud"), "mdl"))
    return jax.shard_map(
        on_device, mesh=mesh, in_specs=in_specs, out_specs=out_specs, check_vma=False
    )
```

time: 1550 us -> 59.5 us (0.04)
  waiting for transfers between devices: 1460 us -> 0 us
  Pallas kernels: 0 us -> 54.6 us
  starting transfers between devices: 41.4 us -> 0 us
    unnamed x3 -> x0, waiting for transfers between devices: 1310 us -> none
    psum x1 -> x0, waiting for transfers between devices: 104 us -> none  [on_device(): error = lax.psum(partial_pred, 'mdl') - goals]
    pallas_call x0 -> x1, Pallas kernels: none -> 54.6 us  [on_device(): pl.pallas_call(functools.partial(kernel, side, teachers, studs), out_shap...]
    all_to_all x5 -> x0, waiting for transfers between devices: 47.7 us -> none  [the longest x1 16.5 us: on_device(): lax.all_to_all(goals_out.reshape(batches, batch_room, action_width), ('te...]
    all_to_all x5 -> x0, starting transfers between devices: 41.3 us -> none  [the longest x1 11 us: on_device(): lax.all_to_all(rows_out.reshape(batches, batch_room, width).astype(jnp.fl...]
  transfers between devices with their start and end apart: 7 -> 0, of which waited for: 7 -> 0; matrix products, arithmetic and copies ran while one was open for 1% -> 0% of each run, Pallas kernels for 0% -> 0%
where the time goes in v1:
time: 59.5 us; the launch traced here: 59.3 us
  Pallas kernels  54.6 us (92%)
  local copies, waits for them, and re-layouts  3.99 us (7%)
  between operations  0.66 us (1%)
    pallas_call x1, Pallas kernels, on_device(): pl.pallas_call(functools.partial(kernel, side, teachers, studs), out_shap...  54.6 us
    unnamed x8, local copies, waits for them, and re-layouts  3.99 us

profile of v1, /device:TPU:1, one launch (start us, length us, event | category | flops | bytes accessed | tf_op | source)
XLA Modules:
  0.0 59.3 jit_solution(12039746301255931680)
XLA Ops:
  0.6 0.0 copy-start.1
  0.6 1.4 %copy.9.tasks = s32[128,1]{1,0:T(8,128)} copy(s32[128,1]{0,1:T(1,128)} %param.8) | data formatting | bytes 1024 | tf_op args[1]
  2.0 0.0 copy-done.1
  2.0 0.7 %copy.10.batches = s32[128,1]{1,0:T(8,128)} copy(s32[128,1]{0,1:T(1,128)S(1)} %copy-done.1) | data formatting | bytes 1024 | tf_op args[2]
  2.8 54.6 %shard_map.86 = (f32[4,256]{1,0:T(4,128)}, f32[4,256]{1,0:T(4,128)}) custom-call(bf16[128,512]{1,0:T(8,128)(2,1)} %states.1, s32[128,1]{1,0:T(8,128)} %copy.9.tasks, s32[128,1]{1,0:T(8,128)} %copy.10.batches, bf16[1,512,256]{2,1,0:T(8,128)(2,1)} %teach_in.1, bf16[1,256,512]{2,1,0:T(8,128)(2,1)} %teach_out.1, bf16[512,256]{1,0:T(8,128)(2,1)} %up.1, ...), custom_call_target="tpu_custom_call" | custom-call | tf_op jit(solution)/shard_map/pallas_call | solution.py:307
  57.4 0.0 copy-start
  57.4 1.3 %copy.13 = f32[4,256]{1,0:T(4,128)} copy(f32[4,256]{1,0:T(4,128)} %get-tuple-element.4) | data formatting | bytes 8192
  58.7 0.0 copy-done
  58.7 0.6 copy.14
Async XLA Ops:
  0.6 1.4 %copy-start.1 = (s32[128,1]{0,1:T(1,128)S(1)}, s32[128,1]{0,1:T(1,128)}, u32[]{:S(2)}) copy-start(s32[128,1]{0,1:T(1,128)} %param.9) | copy-start | bytes 1540
  57.4 1.3 %copy-start = (f32[4,256]{1,0:T(4,128)S(1)}, f32[4,256]{1,0:T(4,128)}, u32[]{:S(2)}) copy-start(f32[4,256]{1,0:T(4,128)} %get-tuple-element.5) | copy-start | bytes 12292

commit v2 on v1

--- a/solution.py
+++ b/solution.py
@@ -40,15 +40,19 @@
     side,
     teachers,
     studs,
-    states,
+    states_hbm,
     tasks,
     batches,
+    teach_in_hbm,
+    teach_out_hbm,
+    up_hbm,
+    down_hbm,
+    grads,
+    states,
     teach_in,
     teach_out,
     up,
     down,
-    grad_up,
-    grad_down,
     out,
     got,
     x,
@@ -66,6 +70,7 @@
     part_in,
     last_out,
     last_in,
+    load_s,
     go_s,
     go_r,
     sum_s,
@@ -114,21 +119,28 @@
         )
         return copy
 
-    hot = jnp.where(tasks[...] == iota((rows, teachers), 1), 1.0, 0.0)
-    lower = onehot(iota((rows, rows), 0) > iota((rows, rows), 1))
-    before = jnp.sum(dot(lower, hot.astype(BF16)) * hot, axis=1, keepdims=True)
-    slot = tasks[...].astype(F32) * BLOCK + before
-    slot = jnp.transpose(jnp.broadcast_to(slot, (rows, rows)))[0:1, :].astype(I32)
+    loads = []
+    for index, (source, held) in enumerate(
+        ((states_hbm, states), (teach_in_hbm, teach_in), (up_hbm, up), (down_hbm, down), (teach_out_hbm, teach_out))
+    ):
+        loads.append(pltpu.make_async_copy(source, held, load_s.at[index]))
+        loads[-1].start()
+
+    hot = jnp.where(tasks[...] == iota((teachers, rows), 0), 1.0, 0.0)
+    earlier = onehot(iota((rows, rows), 0) < iota((rows, rows), 1))
+    before = jnp.sum(dot(hot.astype(BF16), earlier) * hot, axis=0, keepdims=True)
+    slot = tasks[...] * BLOCK + before.astype(I32)
     note = ((slot >> 4) * BLOCK + ROOM + 1 + ((slot & 15) >> 2)) * 4 + (slot & 3)
     place = iota((slots, rows), 0)
-    batch_hot = onehot(batches[...] == iota((rows, LANES), 1))
+    batch_hot = onehot(batches[...] == iota((LANES, rows), 0))
     dispatch = onehot(place == slot)
+    loads[0].wait()
     for piece in range(pieces):
         noted = place * 4 + piece == note
         if piece == 0:
             noted = noted | ((place & 15) == ROOM)
         cols = slice(piece * LANES, (piece + 1) * LANES)
-        block = dot(dispatch, states[:, cols]) + dot(onehot(noted), batch_hot)
+        block = dot(dispatch, states[:, cols]) + dot(onehot(noted), batch_hot, 1, 1)
         out[:, :, cols] = block.astype(BF16).reshape(teachers, BLOCK, LANES)
 
     pl.semaphore_wait(barrier, teachers - 1 + studs - 1 + 2)
@@ -152,6 +164,8 @@
         copy.wait_recv()
 
     arrived = got[...].reshape(slots, width)
+    for load in loads[1:]:
+        load.wait()
     x[...] = dot(keep, arrived).astype(BF16)
     hid[...] = silu(dot(x[...], teach_in[0])).astype(BF16)
     pre[...] = dot(x[...], up[...])
@@ -280,10 +294,12 @@
     for copy in lasts:
         copy.wait_recv()
     total = jnp.sum(last_in[...].astype(F32), axis=0)
-    mine = grad_up.shape[0]
-    even = jnp.full(grad_up.shape, me_s % 2, I32) == 0
-    grad_up[...] = jnp.where(even, total[0:mine], total[mine : 2 * mine])
-    grad_down[...] = jnp.where(even, total[2 * mine : 3 * mine], total[3 * mine : 4 * mine])
+    mine = grads.shape[0] // 2
+    even = jnp.full((mine, grads.shape[1]), me_s % 2, I32) == 0
+    grads[0:mine] = jnp.where(even, total[0:mine], total[mine : 2 * mine])
+    grads[mine : 2 * mine] = jnp.where(
+        even, total[2 * mine : 3 * mine], total[3 * mine : 4 * mine]
+    )
 
     for copy in going + firsts + hists + seconds + lasts:
         copy.wait_send()
@@ -302,14 +318,19 @@
         slots, used = teachers * BLOCK, teachers * ROOM
         mine = width // (teachers * studs)
         vmem = pl.BlockSpec(memory_space=pltpu.VMEM)
-        result = jax.ShapeDtypeStruct((mine, part), F32)
         dma = pltpu.SemaphoreType.DMA
-        return pl.pallas_call(
+        hbm = pl.BlockSpec(memory_space=pl.ANY)
+        grads = pl.pallas_call(
             functools.partial(kernel, side, teachers, studs),
-            out_shape=(result, result),
-            in_specs=[vmem] * 7,
-            out_specs=(vmem, vmem),
+            out_shape=jax.ShapeDtypeStruct((2 * mine, part), F32),
+            in_specs=[hbm, vmem, vmem, hbm, hbm, hbm, hbm],
+            out_specs=vmem,
             scratch_shapes=[
+                pltpu.VMEM(states.shape, BF16),
+                pltpu.VMEM(teach_in.shape, BF16),
+                pltpu.VMEM(teach_out.shape, BF16),
+                pltpu.VMEM(up.shape, BF16),
+                pltpu.VMEM(down.shape, BF16),
                 pltpu.VMEM((teachers, BLOCK, width), BF16),
                 pltpu.VMEM((teachers, BLOCK, width), BF16),
                 pltpu.VMEM((used, width), BF16),
@@ -327,6 +348,7 @@
                 pltpu.VMEM((2, teachers, width // teachers, part), BF16),
                 pltpu.VMEM((studs // 2, 4 * mine, part), BF16),
                 pltpu.VMEM((studs, 4 * mine, part), BF16),
+                dma((5,)),
                 dma((teachers,)),
                 dma((teachers,)),
                 dma((2, 4)),
@@ -339,7 +361,16 @@
                 dma((studs,)),
             ],
             compiler_params=pltpu.CompilerParams(collective_id=0, has_side_effects=True),
-        )(states, tasks, batches, teach_in, teach_out, up, down)
+        )(
+            states,
+            tasks.reshape(1, -1),
+            batches.reshape(1, -1),
+            teach_in,
+            teach_out,
+            up,
+            down,
+        )
+        return grads[:mine], grads[mine:]
 
     in_specs = (
         P(("teach", "stud"), None),

time: 59.5 us -> 56.2 us (0.945)
  local copies, waits for them, and re-layouts: 3.99 us -> 1.37 us
  Pallas kernels: 54.6 us -> 54 us
    unnamed x8 -> x0, local copies, waits for them, and re-layouts: 3.99 us -> none
    slice x0 -> x1, local copies, waits for them, and re-layouts: none -> 1.37 us  [on_device(): return (grads[:mine], grads[mine:])]
    pallas_call x1, Pallas kernels: 54.6 us -> 54 us  [on_device(): pl.pallas_call(functools.partial(kernel, side, teachers, studs), out_shap...]
where the time goes in v2:
time: 56.2 us; the launch traced here: 56 us
  Pallas kernels  54 us (96%)
  local copies, waits for them, and re-layouts  1.37 us (2%)
  between operations  0.64 us (1%)
    pallas_call x1, Pallas kernels, on_device(): pl.pallas_call(functools.partial(kernel, side, teachers, studs), out_shap...  54 us
    slice x1, local copies, waits for them, and re-layouts, on_device(): return (grads[:mine], grads[mine:])  1.37 us

profile of v2, /device:TPU:1, one launch (start us, length us, event | category | flops | bytes accessed | tf_op | source)
XLA Modules:
  0.0 56.0 jit_solution(17615601622889080385)
XLA Ops:
  0.6 54.0 %shard_map.86 = f32[8,256]{1,0:T(8,128)} custom-call(bf16[128,512]{1,0:T(8,128)(2,1)} %states_hbm.1, s32[1,128]{1,0:T(1,128)} %bitcast.2, s32[1,128]{1,0:T(1,128)} %bitcast.3, bf16[1,512,256]{2,1,0:T(8,128)(2,1)} %teach_in_hbm.1, bf16[1,256,512]{2,1,0:T(8,128)(2,1)} %teach_out_hbm.1, bf16[512,256]{1,0:T(8,128)(2,1)} %up_hbm.1, bf16[512,256]{1,0:T(8,128)(2,1)} %down_hbm.1), custom_call_target="tpu_custom_call" | custom-call | tf_op jit(solution)/shard_map/pallas_call | solution.py:323
  54.6 1.4 %fusion = (f32[4,256]{1,0:T(4,128)}, f32[4,256]{1,0:T(4,128)}) fusion(f32[8,256]{1,0:T(8,128)} %shard_map.86), kind=kLoop, calls=%fused_computation | loop fusion | bytes 16384 | tf_op jit(solution)/shard_map/slice | solution.py:373

commit v3 on v2

--- a/solution.py
+++ b/solution.py
@@ -13,6 +13,7 @@
 ROOM = 12
 BLOCK = 16
 LANES = 128
+PARTS = 4
 
 
 def dot(a, b, ca=1, cb=0):
@@ -41,13 +42,15 @@
     teachers,
     studs,
     states_hbm,
-    tasks,
-    batches,
+    tasks_hbm,
+    batches_hbm,
     teach_in_hbm,
     teach_out_hbm,
     up_hbm,
     down_hbm,
     grads,
+    tasks,
+    batches,
     states,
     teach_in,
     teach_out,
@@ -64,6 +67,9 @@
     first_in,
     second_out,
     second_in,
+    scaled_mid,
+    scaled_end,
+    weight,
     hist_out,
     hist_in,
     part_out,
@@ -87,7 +93,7 @@
     rows, width = states.shape
     slots, used = teachers * BLOCK, teachers * ROOM
     pieces = width // LANES
-    mates = (me_m + 1 - 2 * (me_m % 2), 3 - me_m)
+    mates = ((me_m + 1) % 4, (me_m + 3) % 4)
 
     def hops(step):
         dx, dy = step // side, step % side
@@ -121,20 +127,31 @@
 
     loads = []
     for index, (source, held) in enumerate(
-        ((states_hbm, states), (teach_in_hbm, teach_in), (up_hbm, up), (down_hbm, down), (teach_out_hbm, teach_out))
+        (
+            (tasks_hbm, tasks),
+            (batches_hbm, batches),
+            (states_hbm, states),
+            (teach_in_hbm, teach_in),
+            (up_hbm, up),
+            (down_hbm, down),
+            (teach_out_hbm, teach_out),
+        )
     ):
         loads.append(pltpu.make_async_copy(source, held, load_s.at[index]))
         loads[-1].start()
 
+    earlier = onehot(iota((rows, rows), 0) < iota((rows, rows), 1))
+    place = iota((slots, rows), 0)
+    for load in loads[:2]:
+        load.wait()
+
     hot = jnp.where(tasks[...] == iota((teachers, rows), 0), 1.0, 0.0)
-    earlier = onehot(iota((rows, rows), 0) < iota((rows, rows), 1))
     before = jnp.sum(dot(hot.astype(BF16), earlier) * hot, axis=0, keepdims=True)
     slot = tasks[...] * BLOCK + before.astype(I32)
     note = ((slot >> 4) * BLOCK + ROOM + 1 + ((slot & 15) >> 2)) * 4 + (slot & 3)
-    place = iota((slots, rows), 0)
     batch_hot = onehot(batches[...] == iota((LANES, rows), 0))
     dispatch = onehot(place == slot)
-    loads[0].wait()
+    loads[2].wait()
     for piece in range(pieces):
         noted = place * 4 + piece == note
         if piece == 0:
@@ -164,31 +181,10 @@
         copy.wait_recv()
 
     arrived = got[...].reshape(slots, width)
-    for load in loads[1:]:
+
+    for load in loads[3:]:
         load.wait()
     x[...] = dot(keep, arrived).astype(BF16)
-    hid[...] = silu(dot(x[...], teach_in[0])).astype(BF16)
-    pre[...] = dot(x[...], up[...])
-    act[...] = silu(pre[...]).astype(BF16)
-
-    order, firsts, seconds = [], [], []
-    for turn in range(4):
-        chunk = (my_x * 4 // side + 1 + turn) % 4
-        cols = pl.ds(pl.multiple_of(chunk * LANES, LANES), LANES)
-        order.append((chunk, cols))
-        diff = dot(act[...], down[cols, :], 1, 1) - dot(hid[...], teach_out[0, :, cols])
-        err[turn] = diff
-        first_out[turn] = diff.astype(BF16)
-        copy = send(
-            first_out.at[turn],
-            first_in.at[turn],
-            sum_s.at[0, turn],
-            sum_r.at[0, turn],
-            {"mdl": mates[turn % 2]},
-        )
-        copy.start()
-        firsts.append(copy)
-
     marks = onehot((iota((8, slots), 1) & 15) == ROOM)
     hist_out[...] = dot(marks, arrived[:, :LANES])
     hists = []
@@ -200,32 +196,82 @@
         copy.start()
         hists.append(copy)
     hist_in[me_s] = hist_out[...]
+
+    hid[...] = silu(dot(x[...], teach_in[0])).astype(BF16)
+    pre[...] = dot(x[...], up[...])
+    act[...] = silu(pre[...]).astype(BF16)
+
+    chunks, spans = [], []
+    for role in range(4):
+        chunks.append((me_m + 4 - role + my_x * 4 // side) % 4)
+        spans.append(pl.ds(pl.multiple_of(chunks[role] * LANES, LANES), LANES))
+
+    def diff(role):
+        cols = spans[role]
+        return dot(act[...], down[cols, :], 1, 1) - dot(hid[...], teach_out[0, :, cols])
+
+    parts = [slice(part * used // PARTS, (part + 1) * used // PARTS) for part in range(PARTS)]
+    firsts, seconds, thirds = [], [], []
+    for side_of, role in enumerate((0, 3)):
+        first_out[side_of] = diff(role).astype(BF16)
+    for part, at in enumerate(parts):
+        for side_of in range(2):
+            copy = send(
+                first_out.at[side_of, at],
+                first_in.at[side_of, at],
+                sum_s.at[0, side_of, part],
+                sum_r.at[0, side_of, part],
+                {"mdl": mates[side_of]},
+            )
+            copy.start()
+            firsts.append(copy)
+    for side_of, role in enumerate((1, 2)):
+        err[side_of] = diff(role)
+
     batch_of = jnp.zeros((used, LANES), F32)
     for piece in range(pieces):
         pick = onehot((target == base + (inner - ROOM - 1) * 4 + piece) & (inner > ROOM))
         batch_of += dot(pick, arrived[:, piece * LANES : (piece + 1) * LANES])
     pre[...] = silu_slope(pre[...])
 
-    for turn in range(4):
-        firsts[turn].wait_recv()
-        diff = err[turn] + first_in[turn].astype(F32)
-        err[turn] = diff
-        second_out[turn] = diff.astype(BF16)
-        copy = send(
-            second_out.at[turn],
-            second_in.at[turn],
-            sum_s.at[1, turn],
-            sum_r.at[1, turn],
-            {"mdl": mates[1 - turn % 2]},
-        )
-        copy.start()
-        seconds.append(copy)
+    for part, at in enumerate(parts):
+        for side_of in range(2):
+            firsts[part * 2 + side_of].wait_recv()
+            total = err[side_of, at] + first_in[side_of, at].astype(F32)
+            err[side_of, at] = total
+            second_out[side_of, at] = total.astype(BF16)
+            copy = send(
+                second_out.at[side_of, at],
+                second_in.at[1 - side_of, at],
+                sum_s.at[1, side_of, part],
+                sum_r.at[1, 1 - side_of, part],
+                {"mdl": mates[side_of]},
+            )
+            copy.start()
+            seconds.append(copy)
 
     for copy in hists:
         copy.wait_recv()
     counts = jnp.sum(hist_in[...], axis=0)
     share = jnp.where(counts > 0.0, 2.0 / jnp.maximum(counts, 1.0), 0.0)
-    weight = jnp.sum(batch_of * share[0:1, :], axis=1, keepdims=True)
+    weight[...] = jnp.broadcast_to(
+        jnp.sum(batch_of * share[0:1, :], axis=1, keepdims=True), weight.shape
+    )
+
+    for part, at in enumerate(parts):
+        for side_of in range(2):
+            seconds[part * 2 + 1 - side_of].wait_recv()
+            total = err[side_of, at] + second_in[side_of, at].astype(F32)
+            scaled_mid[side_of, at] = (total * weight[at]).astype(BF16)
+            copy = send(
+                scaled_mid.at[side_of, at],
+                scaled_end.at[side_of, at],
+                sum_s.at[2, side_of, part],
+                sum_r.at[2, side_of, part],
+                {"mdl": mates[1 - side_of]},
+            )
+            copy.start()
+            thirds.append(copy)
 
     def part_copy(kind, to):
         return send(
@@ -239,11 +285,14 @@
     per = teachers // 4
     part_rows = part_out.shape[2]
     back = jnp.zeros((used, up.shape[1]), F32)
-    for turn in range(4):
-        chunk, cols = order[turn]
-        seconds[turn].wait_recv()
-        total = err[turn] + second_in[turn].astype(F32)
-        scaled = (total * weight).astype(BF16)
+    for turn, role in enumerate((1, 2, 0, 3)):
+        chunk, cols, side_of = chunks[role], spans[role], turn % 2
+        if turn < 2:
+            scaled = scaled_mid[side_of]
+        else:
+            for part in range(PARTS):
+                thirds[part * 2 + side_of].wait_recv()
+            scaled = scaled_end[side_of]
         grad = dot(scaled, act[...], 0, 0)
         part_out[1, pl.ds(chunk * per, per)] = grad.astype(BF16).reshape(per, part_rows, -1)
         back += dot(scaled, down[cols, :])
@@ -301,7 +350,7 @@
         even, total[2 * mine : 3 * mine], total[3 * mine : 4 * mine]
     )
 
-    for copy in going + firsts + hists + seconds + lasts:
+    for copy in going + hists + firsts + seconds + thirds + lasts:
         copy.wait_send()
     for step in steps:
         for kind in range(2):
@@ -323,9 +372,11 @@
         grads = pl.pallas_call(
             functools.partial(kernel, side, teachers, studs),
             out_shape=jax.ShapeDtypeStruct((2 * mine, part), F32),
-            in_specs=[hbm, vmem, vmem, hbm, hbm, hbm, hbm],
+            in_specs=[hbm] * 7,
             out_specs=vmem,
             scratch_shapes=[
+                pltpu.VMEM((1, states.shape[0]), I32),
+                pltpu.VMEM((1, states.shape[0]), I32),
                 pltpu.VMEM(states.shape, BF16),
                 pltpu.VMEM(teach_in.shape, BF16),
                 pltpu.VMEM(teach_out.shape, BF16),
@@ -337,22 +388,25 @@
                 pltpu.VMEM((used, part), BF16),
                 pltpu.VMEM((used, part), BF16),
                 pltpu.VMEM((used, part), F32),
-                pltpu.VMEM((4, used, actions // 4), F32),
-                pltpu.VMEM((4, used, actions // 4), BF16),
-                pltpu.VMEM((4, used, actions // 4), BF16),
-                pltpu.VMEM((4, used, actions // 4), BF16),
-                pltpu.VMEM((4, used, actions // 4), BF16),
+                pltpu.VMEM((2, used, actions // 4), F32),
+                pltpu.VMEM((2, used, actions // 4), BF16),
+                pltpu.VMEM((2, used, actions // 4), BF16),
+                pltpu.VMEM((2, used, actions // 4), BF16),
+                pltpu.VMEM((2, used, actions // 4), BF16),
+                pltpu.VMEM((2, used, actions // 4), BF16),
+                pltpu.VMEM((2, used, actions // 4), BF16),
+                pltpu.VMEM((used, LANES), F32),
                 pltpu.VMEM((8, LANES), F32),
                 pltpu.VMEM((studs, 8, LANES), F32),
                 pltpu.VMEM((2, teachers, width // teachers, part), BF16),
                 pltpu.VMEM((2, teachers, width // teachers, part), BF16),
                 pltpu.VMEM((studs // 2, 4 * mine, part), BF16),
                 pltpu.VMEM((studs, 4 * mine, part), BF16),
-                dma((5,)),
+                dma((7,)),
                 dma((teachers,)),
                 dma((teachers,)),
-                dma((2, 4)),
-                dma((2, 4)),
+                dma((3, 2, PARTS)),
+                dma((3, 2, PARTS)),
                 dma((studs,)),
                 dma((studs,)),
                 dma((2, teachers)),

time: 56.2 us -> 54.9 us (0.977)
  Pallas kernels: 54 us -> 52.7 us
    pallas_call x1, Pallas kernels: 54 us -> 52.7 us  [on_device(): pl.pallas_call(functools.partial(kernel, side, teachers, studs), out_shap...]
where the time goes in v3:
time: 54.9 us; the launch traced here: 54.8 us
  Pallas kernels  52.7 us (96%)
  local copies, waits for them, and re-layouts  1.37 us (2%)
  between operations  0.64 us (1%)
    pallas_call x1, Pallas kernels, on_device(): pl.pallas_call(functools.partial(kernel, side, teachers, studs), out_shap...  52.7 us
    slice x1, local copies, waits for them, and re-layouts, on_device(): return (grads[:mine], grads[mine:])  1.37 us

profile of v3, /device:TPU:1, one launch (start us, length us, event | category | flops | bytes accessed | tf_op | source)
XLA Modules:
  0.0 54.8 jit_solution(8180497749313479420)
XLA Ops:
  0.6 52.7 %shard_map.86 = f32[8,256]{1,0:T(8,128)} custom-call(bf16[128,512]{1,0:T(8,128)(2,1)} %states_hbm.1, s32[1,128]{1,0:T(1,128)} %bitcast.2, s32[1,128]{1,0:T(1,128)} %bitcast.3, bf16[1,512,256]{2,1,0:T(8,128)(2,1)} %teach_in_hbm.1, bf16[1,256,512]{2,1,0:T(8,128)(2,1)} %teach_out_hbm.1, bf16[512,256]{1,0:T(8,128)(2,1)} %up_hbm.1, bf16[512,256]{1,0:T(8,128)(2,1)} %down_hbm.1), custom_call_target="tpu_custom_call" | custom-call | tf_op jit(solution)/shard_map/pallas_call | solution.py:372
  53.4 1.4 %fusion = (f32[4,256]{1,0:T(4,128)}, f32[4,256]{1,0:T(4,128)}) fusion(f32[8,256]{1,0:T(8,128)} %shard_map.86), kind=kLoop, calls=%fused_computation | loop fusion | bytes 16384 | tf_op jit(solution)/shard_map/slice | solution.py:427

commit v4 on v3

--- a/solution.py
+++ b/solution.py
@@ -138,7 +138,8 @@
         )
     ):
         loads.append(pltpu.make_async_copy(source, held, load_s.at[index]))
-        loads[-1].start()
+    for load in loads[:3]:
+        load.start()
 
     earlier = onehot(iota((rows, rows), 0) < iota((rows, rows), 1))
     place = iota((slots, rows), 0)
@@ -152,6 +153,8 @@
     batch_hot = onehot(batches[...] == iota((LANES, rows), 0))
     dispatch = onehot(place == slot)
     loads[2].wait()
+    for load in loads[3:]:
+        load.start()
     for piece in range(pieces):
         noted = place * 4 + piece == note
         if piece == 0:
@@ -185,18 +188,6 @@
     for load in loads[3:]:
         load.wait()
     x[...] = dot(keep, arrived).astype(BF16)
-    marks = onehot((iota((8, slots), 1) & 15) == ROOM)
-    hist_out[...] = dot(marks, arrived[:, :LANES])
-    hists = []
-    for step in range(1, studs):
-        to = (me_s + step) % studs
-        copy = send(
-            hist_out, hist_in.at[me_s], hist_s.at[step], hist_r.at[step], {"stud": to}
-        )
-        copy.start()
-        hists.append(copy)
-    hist_in[me_s] = hist_out[...]
-
     hid[...] = silu(dot(x[...], teach_in[0])).astype(BF16)
     pre[...] = dot(x[...], up[...])
     act[...] = silu(pre[...]).astype(BF16)
@@ -228,6 +219,18 @@
     for side_of, role in enumerate((1, 2)):
         err[side_of] = diff(role)
 
+    marks = onehot((iota((8, slots), 1) & 15) == ROOM)
+    hist_out[...] = dot(marks, arrived[:, :LANES])
+    hists = []
+    for step in range(1, studs):
+        to = (me_s + step) % studs
+        copy = send(
+            hist_out, hist_in.at[me_s], hist_s.at[step], hist_r.at[step], {"stud": to}
+        )
+        copy.start()
+        hists.append(copy)
+    hist_in[me_s] = hist_out[...]
+
     batch_of = jnp.zeros((used, LANES), F32)
     for piece in range(pieces):
         pick = onehot((target == base + (inner - ROOM - 1) * 4 + piece) & (inner > ROOM))
@@ -304,10 +307,18 @@
                 part_copy(1, to).start()
 
     pre_grad = (back * pre[...]).astype(BF16)
-    grad = dot(x[...], pre_grad, 0, 0)
-    part_out[0] = grad.astype(BF16).reshape(teachers, part_rows, -1)
-    for step in steps:
-        part_copy(0, peer(step)).start()
+    for turn in (2, 1, 3, 0):
+        block = (my_x + turn * side // 4) % 4
+        cols = pl.ds(pl.multiple_of(block * LANES, LANES), LANES)
+        grad = dot(x[:, cols], pre_grad, 0, 0)
+        part_out[0, pl.ds(block * per, per)] = grad.astype(BF16).reshape(per, part_rows, -1)
+        for piece in range(per):
+            to = block * per + (my_y + piece) % per
+
+            @pl.when(to != me_t)
+            def _():
+                part_copy(0, to).start()
+
     part_in[1, me_t] = part_out[1, me_t]
     part_in[0, me_t] = part_out[0, me_t]
 
@@ -371,7 +382,7 @@
         hbm = pl.BlockSpec(memory_space=pl.ANY)
         grads = pl.pallas_call(
             functools.partial(kernel, side, teachers, studs),
-            out_shape=jax.ShapeDtypeStruct((2 * mine, part), F32),
+            out_shape=pltpu.VMEM((2 * mine, part), F32),
             in_specs=[hbm] * 7,
             out_specs=vmem,
             scratch_shapes=[

time: 54.9 us -> 54.2 us (0.987)
  local copies, waits for them, and re-layouts: 1.37 us -> 0.6 us
    slice x1, local copies, waits for them, and re-layouts: 1.37 us -> 0.6 us  [on_device(): return (grads[:mine], grads[mine:])]
where the time goes in v4:
time: 54.2 us; the launch traced here: 54 us
  Pallas kernels  52.8 us (97%)
  between operations  0.64 us (1%)
  local copies, waits for them, and re-layouts  0.6 us (1%)
    pallas_call x1, Pallas kernels, on_device(): pl.pallas_call(functools.partial(kernel, side, teachers, studs), out_shap...  52.8 us

profile of v4, /device:TPU:1, one launch (start us, length us, event | category | flops | bytes accessed | tf_op | source)
XLA Modules:
  0.0 54.0 jit_solution(14799356669701687819)
XLA Ops:
  0.6 52.8 %shard_map.86 = f32[8,256]{1,0:T(8,128)S(1)} custom-call(bf16[128,512]{1,0:T(8,128)(2,1)} %states_hbm.1, s32[1,128]{1,0:T(1,128)} %bitcast.2, s32[1,128]{1,0:T(1,128)} %bitcast.3, bf16[1,512,256]{2,1,0:T(8,128)(2,1)} %teach_in_hbm.1, bf16[1,256,512]{2,1,0:T(8,128)(2,1)} %teach_out_hbm.1, bf16[512,256]{1,0:T(8,128)(2,1)} %up_hbm.1, bf16[512,256]{1,0:T(8,128)(2,1)} %down_hbm.1), custom_call_target="tpu_custom_call" | custom-call | tf_op jit(solution)/shard_map/pallas_call | solution.py:383
  53.4 0.6 %fusion = (f32[4,256]{1,0:T(4,128)}, f32[4,256]{1,0:T(4,128)}) fusion(f32[8,256]{1,0:T(8,128)S(1)} %shard_map.86), kind=kLoop, calls=%fused_computation | loop fusion | bytes 16384 | tf_op jit(solution)/shard_map/slice | solution.py:438

commit v5 on v4

--- a/solution.py
+++ b/solution.py
@@ -72,6 +72,8 @@
     weight,
     hist_out,
     hist_in,
+    sums_out,
+    sums_in,
     part_out,
     part_in,
     last_out,
@@ -83,6 +85,8 @@
     sum_r,
     hist_s,
     hist_r,
+    sums_s,
+    sums_r,
     part_s,
     part_r,
     last_s,
@@ -151,14 +155,13 @@
     slot = tasks[...] * BLOCK + before.astype(I32)
     note = ((slot >> 4) * BLOCK + ROOM + 1 + ((slot & 15) >> 2)) * 4 + (slot & 3)
     batch_hot = onehot(batches[...] == iota((LANES, rows), 0))
+    hist_out[...] = dot(jnp.ones((8, rows), BF16), batch_hot, 1, 1)
     dispatch = onehot(place == slot)
     loads[2].wait()
     for load in loads[3:]:
         load.start()
     for piece in range(pieces):
         noted = place * 4 + piece == note
-        if piece == 0:
-            noted = noted | ((place & 15) == ROOM)
         cols = slice(piece * LANES, (piece + 1) * LANES)
         block = dot(dispatch, states[:, cols]) + dot(onehot(noted), batch_hot, 1, 1)
         out[:, :, cols] = block.astype(BF16).reshape(teachers, BLOCK, LANES)
@@ -174,6 +177,15 @@
         copy.start()
         going.append(copy)
     got[me_t] = out[me_t]
+    hists = []
+    for step in range(1, studs):
+        to = (me_s + step) % studs
+        copy = send(
+            hist_out, hist_in.at[me_s], hist_s.at[step], hist_r.at[step], {"stud": to}
+        )
+        copy.start()
+        hists.append(copy)
+    hist_in[me_s] = hist_out[...]
 
     source = iota((used, slots), 1)
     target = iota((used, slots), 0)
@@ -219,18 +231,17 @@
     for side_of, role in enumerate((1, 2)):
         err[side_of] = diff(role)
 
-    marks = onehot((iota((8, slots), 1) & 15) == ROOM)
-    hist_out[...] = dot(marks, arrived[:, :LANES])
-    hists = []
-    for step in range(1, studs):
-        to = (me_s + step) % studs
+    for copy in hists:
+        copy.wait_recv()
+    sums_out[...] = jnp.sum(hist_in[...], axis=0)
+    sums = []
+    for step in steps:
         copy = send(
-            hist_out, hist_in.at[me_s], hist_s.at[step], hist_r.at[step], {"stud": to}
+            sums_out, sums_in.at[me_t], sums_s.at[step], sums_r.at[step], {"teach": peer(step)}
         )
         copy.start()
-        hists.append(copy)
-    hist_in[me_s] = hist_out[...]
-
+        sums.append(copy)
+    sums_in[me_t] = sums_out[...]
     batch_of = jnp.zeros((used, LANES), F32)
     for piece in range(pieces):
         pick = onehot((target == base + (inner - ROOM - 1) * 4 + piece) & (inner > ROOM))
@@ -253,9 +264,9 @@
             copy.start()
             seconds.append(copy)
 
-    for copy in hists:
+    for copy in sums:
         copy.wait_recv()
-    counts = jnp.sum(hist_in[...], axis=0)
+    counts = jnp.sum(sums_in[...], axis=0)
     share = jnp.where(counts > 0.0, 2.0 / jnp.maximum(counts, 1.0), 0.0)
     weight[...] = jnp.broadcast_to(
         jnp.sum(batch_of * share[0:1, :], axis=1, keepdims=True), weight.shape
@@ -337,12 +348,18 @@
     chips = studs // 2
     sum_down = part_wait(1).reshape(chips, part_rows // chips, -1)
     sum_up = part_wait(0).reshape(chips, part_rows // chips, -1)
-    last_out[...] = jnp.concatenate([sum_up, sum_down], axis=1).astype(BF16)
+    mine = grads.shape[0] // 2
+    for core in range(2):
+        at = slice(core * mine, (core + 1) * mine)
+        rows8 = jnp.concatenate([sum_up[:, at], sum_down[:, at]], axis=1)
+        last_out[:, core] = jnp.concatenate(
+            [rows8[:, :, :LANES], rows8[:, :, LANES:]], axis=1
+        ).astype(BF16)
     lasts = []
     for step in range(1, studs):
         to = (me_s + step) % studs
         copy = send(
-            last_out.at[to // 2],
+            last_out.at[to // 2, to % 2],
             last_in.at[me_s],
             last_s.at[step],
             last_r.at[step],
@@ -350,18 +367,14 @@
         )
         copy.start()
         lasts.append(copy)
-    last_in[me_s] = last_out[me_s // 2]
+    last_in[me_s] = last_out[me_s // 2, me_s % 2]
     for copy in lasts:
         copy.wait_recv()
     total = jnp.sum(last_in[...].astype(F32), axis=0)
-    mine = grads.shape[0] // 2
-    even = jnp.full((mine, grads.shape[1]), me_s % 2, I32) == 0
-    grads[0:mine] = jnp.where(even, total[0:mine], total[mine : 2 * mine])
-    grads[mine : 2 * mine] = jnp.where(
-        even, total[2 * mine : 3 * mine], total[3 * mine : 4 * mine]
-    )
-
-    for copy in going + hists + firsts + seconds + thirds + lasts:
+    grads[:, :LANES] = total[: 2 * mine]
+    grads[:, LANES:] = total[2 * mine :]
+
+    for copy in going + hists + sums + firsts + seconds + thirds + lasts:
         copy.wait_send()
     for step in steps:
         for kind in range(2):
@@ -409,10 +422,12 @@
                 pltpu.VMEM((used, LANES), F32),
                 pltpu.VMEM((8, LANES), F32),
                 pltpu.VMEM((studs, 8, LANES), F32),
+                pltpu.VMEM((8, LANES), F32),
+                pltpu.VMEM((teachers, 8, LANES), F32),
                 pltpu.VMEM((2, teachers, width // teachers, part), BF16),
                 pltpu.VMEM((2, teachers, width // teachers, part), BF16),
-                pltpu.VMEM((studs // 2, 4 * mine, part), BF16),
-                pltpu.VMEM((studs, 4 * mine, part), BF16),
+                pltpu.VMEM((studs // 2, 2, 4 * mine, part // 2), BF16),
+                pltpu.VMEM((studs, 4 * mine, part // 2), BF16),
                 dma((7,)),
                 dma((teachers,)),
                 dma((teachers,)),
@@ -420,6 +435,8 @@
                 dma((3, 2, PARTS)),
                 dma((studs,)),
                 dma((studs,)),
+                dma((teachers,)),
+                dma((teachers,)),
                 dma((2, teachers)),
                 dma((2, teachers)),
                 dma((studs,)),

time: 54.2 us -> 53.3 us (0.983)
  Pallas kernels: 52.8 us -> 51.9 us
    pallas_call x1, Pallas kernels: 52.8 us -> 51.9 us  [on_device(): pl.pallas_call(functools.partial(kernel, side, teachers, studs), out_shap...]
where the time goes in v5:
time: 53.3 us; the launch traced here: 53.1 us
  Pallas kernels  51.9 us (97%)
  between operations  0.64 us (1%)
  local copies, waits for them, and re-layouts  0.6 us (1%)
    pallas_call x1, Pallas kernels, on_device(): pl.pallas_call(functools.partial(kernel, side, teachers, studs), out_shap...  51.9 us

profile of v5, /device:TPU:1, one launch (start us, length us, event | category | flops | bytes accessed | tf_op | source)
XLA Modules:
  0.0 53.1 jit_solution(2912722904293503424)
XLA Ops:
  0.6 51.9 %shard_map.86 = f32[8,256]{1,0:T(8,128)S(1)} custom-call(bf16[128,512]{1,0:T(8,128)(2,1)} %states_hbm.1, s32[1,128]{1,0:T(1,128)} %bitcast.2, s32[1,128]{1,0:T(1,128)} %bitcast.3, bf16[1,512,256]{2,1,0:T(8,128)(2,1)} %teach_in_hbm.1, bf16[1,256,512]{2,1,0:T(8,128)(2,1)} %teach_out_hbm.1, bf16[512,256]{1,0:T(8,128)(2,1)} %up_hbm.1, bf16[512,256]{1,0:T(8,128)(2,1)} %down_hbm.1), custom_call_target="tpu_custom_call" | custom-call | tf_op jit(solution)/shard_map/pallas_call | solution.py:396
  52.5 0.6 %fusion = (f32[4,256]{1,0:T(4,128)}, f32[4,256]{1,0:T(4,128)}) fusion(f32[8,256]{1,0:T(8,128)S(1)} %shard_map.86), kind=kLoop, calls=%fused_computation | loop fusion | bytes 16384 | tf_op jit(solution)/shard_map/slice | solution.py:455

commit v6 on v5

--- a/solution.py
+++ b/solution.py
@@ -217,8 +217,7 @@
     firsts, seconds, thirds = [], [], []
     for side_of, role in enumerate((0, 3)):
         first_out[side_of] = diff(role).astype(BF16)
-    for part, at in enumerate(parts):
-        for side_of in range(2):
+        for part, at in enumerate(parts):
             copy = send(
                 first_out.at[side_of, at],
                 first_in.at[side_of, at],
@@ -250,7 +249,7 @@
 
     for part, at in enumerate(parts):
         for side_of in range(2):
-            firsts[part * 2 + side_of].wait_recv()
+            firsts[side_of * PARTS + part].wait_recv()
             total = err[side_of, at] + first_in[side_of, at].astype(F32)
             err[side_of, at] = total
             second_out[side_of, at] = total.astype(BF16)

time: 53.3 us -> 53.4 us (level)
  no operation moved by 1% of the time
where the time goes in v6:
time: 53.4 us; the launch traced here: 53.3 us
  Pallas kernels  52 us (97%)
  between operations  0.64 us (1%)
  local copies, waits for them, and re-layouts  0.6 us (1%)
    pallas_call x1, Pallas kernels, on_device(): pl.pallas_call(functools.partial(kernel, side, teachers, studs), out_shap...  52 us

profile of v6, /device:TPU:1, one launch (start us, length us, event | category | flops | bytes accessed | tf_op | source)
XLA Modules:
  0.0 53.3 jit_solution(7329711710109002459)
XLA Ops:
  0.6 52.0 %shard_map.86 = f32[8,256]{1,0:T(8,128)S(1)} custom-call(bf16[128,512]{1,0:T(8,128)(2,1)} %states_hbm.1, s32[1,128]{1,0:T(1,128)} %bitcast.2, s32[1,128]{1,0:T(1,128)} %bitcast.3, bf16[1,512,256]{2,1,0:T(8,128)(2,1)} %teach_in_hbm.1, bf16[1,256,512]{2,1,0:T(8,128)(2,1)} %teach_out_hbm.1, bf16[512,256]{1,0:T(8,128)(2,1)} %up_hbm.1, bf16[512,256]{1,0:T(8,128)(2,1)} %down_hbm.1), custom_call_target="tpu_custom_call" | custom-call | tf_op jit(solution)/shard_map/pallas_call | solution.py:395
  52.7 0.6 %fusion = (f32[4,256]{1,0:T(4,128)}, f32[4,256]{1,0:T(4,128)}) fusion(f32[8,256]{1,0:T(8,128)S(1)} %shard_map.86), kind=kLoop, calls=%fused_computation | loop fusion | bytes 16384 | tf_op jit(solution)/shard_map/slice | solution.py:454
